TPU v7x, 256 devices: a whole 4x4x8 slice. The times are simulated.
256 devices in a mesh: leaf: 64 (over y, z, core), grid: 4 (over x).
Axes of the slice: x: 4, y: 4, z: 8, core: 2. Of those that a mesh axis runs over, the one named last changes fastest.
Arguments:
- rhs: bfloat16 [5, 128, 256, 256], P(None, 'leaf', 'grid'), may hold values from -6 to 6
- fwd_inv: bfloat16 [5, 128, 256, 256], P(None, 'leaf', 'grid')
- bwd_inv: bfloat16 [5, 128, 256, 256], P(None, 'leaf', 'grid')
- upd_t: bfloat16 [4, 128, 256, 512], P(None, 'leaf', 'grid'), may hold values from -0.25 to 0.25
- bwd_t: bfloat16 [4, 128, 512, 256], P(None, 'leaf', 'grid'), may hold values from -0.1875 to 0.1875
- dest_owner: int32 [4, 64, 4, 256, 1], P(None, 'leaf', 'grid'), may hold values from 0 to 63; in each aligned block of 256 rows (0 to 255, 256 to 511, ..., all dimensions but the last counted through in order) at most 10 rows name the same one
- dest_row: int32 [4, 64, 4, 256], P(None, 'leaf', 'grid'), may hold values from 128 to 639, as said below
Outputs:
- solution: bfloat16 [5, 128, 256, 256], P(None, 'leaf', 'grid')
Inputs may be any that keep to these rules, and one draw needn't show every extreme that they name: `dest_owner`: in the rows of one device at one level (one aligned block of 256), no owner is named more than 10 times, a bound that some block reaches. `dest_row`: an entry of level l reaches a row of a later level: it lies from (l + 1) * 2 * 64 to 639.
All inputs are finite; a program needn't handle non-finite values.
Results may differ from a plain program's by a relative error of at most 0.025.
Values may be sent and summed in bfloat16 or wider, within the bound.
A program may use at most 64 MiB of HBM per device.

v0:
```python
import jax
import jax.numpy as jnp
from jax import lax
from jax.sharding import PartitionSpec as P


def apply_inverse(inverse_rows, block_bf):
    return jnp.einsum(
        "kiw,kwn->kin",
        inverse_rows,
        lax.all_gather(block_bf, "grid", axis=1, tiled=True),
        preferred_element_type=jnp.float32,
    )


def grid_reduce(term_fn, kept_rows):
    return lax.psum_scatter(
        term_fn(jnp.int32(0), kept_rows * lax.axis_size("grid")).astype(jnp.bfloat16),
        "grid",
        scatter_dimension=0,
        tiled=True,
    ).astype(jnp.float32)


def send_back(solved_rows):
    return lax.all_to_all(solved_rows, "leaf", split_axis=0, concat_axis=0, tiled=True)


def local(rhs, fwd_inv, bwd_inv, upd_t, bwd_t, dest_owner, dest_row):
    levels, per_level, grid_rows, columns = rhs.shape
    group_rows = bwd_t.shape[2]
    owners = lax.axis_size("leaf")
    capacity = max(2, 8 * per_level * group_rows // (3 * owners))
    block_rows = per_level * grid_rows
    leaf_ids = jnp.arange(owners, dtype=jnp.int32)
    accum = rhs.astype(jnp.float32).reshape(levels * block_rows, columns)

    def placement(level):
        owner_ids = dest_owner[level].reshape(-1)
        targets = dest_row[level].reshape(-1)
        onehot = (owner_ids[:, None] == leaf_ids[None, :]).astype(jnp.int32)
        before = jnp.cumsum(onehot, axis=0) - onehot
        slot_in = jnp.sum(before * onehot, axis=1)
        return (owner_ids * capacity + slot_in, targets)

    forward_out = []
    kept_index = []
    for level in range(levels):
        block = accum[level * block_rows : (level + 1) * block_rows].reshape(
            per_level, grid_rows, columns
        )
        block_bf = block.astype(jnp.bfloat16)
        solved = apply_inverse(fwd_inv[level], block_bf)
        forward_out.append(solved)
        if level < levels - 1:
            lowered = solved.astype(jnp.bfloat16)

            def forward_term(offset, length, lower_cols=upd_t[level], lowered=lowered):
                return jnp.einsum(
                    "kwr,kwn->rkn", lower_cols, lowered, preferred_element_type=jnp.float32
                )

            summed = grid_reduce(forward_term, group_rows)
            routed = summed.reshape(group_rows * per_level, columns)
            slot_pos, targets = placement(level)
            outgoing = jnp.zeros((owners * capacity, columns), jnp.float32).at[slot_pos].set(routed)
            outgoing_index = jnp.zeros((owners * capacity,), jnp.int32).at[slot_pos].set(targets)
            incoming, incoming_index = (
                lax.all_to_all(
                    outgoing.reshape(owners, capacity, columns).astype(jnp.bfloat16),
                    "leaf",
                    split_axis=0,
                    concat_axis=0,
                    tiled=True,
                ).astype(jnp.float32),
                lax.all_to_all(
                    outgoing_index.reshape(owners, capacity),
                    "leaf",
                    split_axis=0,
                    concat_axis=0,
                    tiled=True,
                ),
            )
            accum = accum.at[incoming_index.reshape(-1)].add(-incoming.reshape(-1, columns))
            kept_index.append(incoming_index)
    solution = jnp.zeros((levels * block_rows, columns), jnp.bfloat16)
    for level in reversed(range(levels)):
        reduced = forward_out[level]
        if level < levels - 1:
            slot_pos, targets = placement(level)
            asking = (
                jnp.zeros((owners * capacity,), jnp.int32)
                .at[slot_pos]
                .set(targets)
                .reshape(owners, capacity)
            )

            def answer(asked, solution=solution):
                found = solution[asked.reshape(-1)].reshape(asked.shape[0], asked.shape[1], columns)
                return send_back(found)

            returned = answer(
                lax.all_to_all(asking, "leaf", split_axis=0, concat_axis=0, tiled=True)
            )
            pulled = returned.reshape(owners * capacity, columns)[slot_pos].reshape(
                group_rows, per_level, columns
            )

            def backward_term(offset, length, upper_rows=bwd_t[level], pulled=pulled):
                return jnp.einsum(
                    "kjw,jkn->wkn", upper_rows, pulled, preferred_element_type=jnp.float32
                )

            upper_sum = grid_reduce(backward_term, grid_rows)
            reduced = reduced - jnp.swapaxes(upper_sum, 0, 1)
        result = apply_inverse(bwd_inv[level], reduced.astype(jnp.bfloat16))
        solution = solution.at[level * block_rows : (level + 1) * block_rows].set(
            result.astype(jnp.bfloat16).reshape(block_rows, columns)
        )
    return solution.reshape(levels, per_level, grid_rows, columns)


def solution(mesh):
    placed = (
        P(None, "leaf", "grid", None),
        P(None, "leaf", "grid", None),
        P(None, "leaf", "grid", None),
        P(None, "leaf", "grid", None),
        P(None, "leaf", "grid", None),
        P(None, "leaf", "grid", None, None),
        P(None, "leaf", "grid", None),
    )
    return jax.shard_map(
        local, mesh=mesh, in_specs=placed, out_specs=P(None, "leaf", "grid", None), check_vma=False
    )
```

profile of v0, /device:TPU:8, one launch (start us, length us, event | category | flops | bytes accessed | tf_op | source)
XLA Modules:
  0.0 601.4 jit_solution(17086478699634533320)
XLA Ops:
  7.4 12.6 %all-gather = bf16[1,2,256,256]{3,2,1,0:T(8,128)(2,1)S(1)} all-gather(bf16[1,2,64,256]{3,2,1,0:T(8,128)(2,1)S(1)} %slice-done), channel_id=2, replica_groups=mesh['leaf'=64,'grid'=4] {'grid'}, dimensions={2}, use_global_device_ids=true | all-gather | bytes 327680 | tf_op jit(solution)/shard_map/all_gather | solution.py:11
  33.2 12.1 %all-to-all-start = ((s32[64,1,10]{2,1,0:T(1,128)}), s32[64,1,10]{2,1,0:T(1,128)S(1)}, u32[]{:S(2)}, u32[]{:S(2)}) async-start(s32[64,1,10]{2,1,0:T(1,128)} %bitcast.8), calls=%async_computation | async-start | bytes 65536 | tf_op jit(solution)/shard_map/all_to_all | solution.py:76
  65.1 15.1 %all-to-all-done.1 = bf16[64,10,256]{2,1,0:T(8,128)(2,1)S(1)} async-done(((bf16[64,10,256]{2,1,0:T(8,128)(2,1)}), bf16[64,10,256]{2,1,0:T(8,128)(2,1)S(1)}, u32[]{:S(2)}, u32[]{:S(2)}) %all-to-all-start.1) | async-done | bytes 327712 | tf_op jit(solution)/shard_map/all_to_all | solution.py:69
  86.9 12.5 %all_gather.31 = bf16[2,256,256]{2,1,0:T(8,128)(2,1)S(1)} all-gather(bf16[2,64,256]{2,1,0:T(8,128)(2,1)S(1)} %bitcast.266), channel_id=1, replica_groups=mesh['leaf'=64,'grid'=4] {'grid'}, dimensions={1}, use_global_device_ids=true | all-gather | bytes 327680 | tf_op jit(solution)/shard_map/all_gather | solution.py:11
  137.6 15.7 %all-to-all-done.3 = bf16[64,10,256]{2,1,0:T(8,128)(2,1)S(1)} async-done(((bf16[64,10,256]{2,1,0:T(8,128)(2,1)}), bf16[64,10,256]{2,1,0:T(8,128)(2,1)S(1)}, u32[]{:S(2)}, u32[]{:S(2)}) %all-to-all-start.3) | async-done | bytes 327712 | tf_op jit(solution)/shard_map/all_to_all | solution.py:69
  160.0 12.4 %all_gather.32 = bf16[2,256,256]{2,1,0:T(8,128)(2,1)S(1)} all-gather(bf16[2,64,256]{2,1,0:T(8,128)(2,1)S(1)} %bitcast.267), channel_id=1, replica_groups=mesh['leaf'=64,'grid'=4] {'grid'}, dimensions={1}, use_global_device_ids=true | all-gather | bytes 327680 | tf_op jit(solution)/shard_map/all_gather | solution.py:11
  211.2 15.3 %all-to-all-done.5 = bf16[64,10,256]{2,1,0:T(8,128)(2,1)S(1)} async-done(((bf16[64,10,256]{2,1,0:T(8,128)(2,1)}), bf16[64,10,256]{2,1,0:T(8,128)(2,1)S(1)}, u32[]{:S(2)}, u32[]{:S(2)}) %all-to-all-start.5) | async-done | bytes 327712 | tf_op jit(solution)/shard_map/all_to_all | solution.py:69
  233.1 12.4 %all_gather.33 = bf16[2,256,256]{2,1,0:T(8,128)(2,1)S(1)} all-gather(bf16[2,64,256]{2,1,0:T(8,128)(2,1)S(1)} %bitcast.268), channel_id=1, replica_groups=mesh['leaf'=64,'grid'=4] {'grid'}, dimensions={1}, use_global_device_ids=true | all-gather | bytes 327680 | tf_op jit(solution)/shard_map/all_gather | solution.py:11
  257.1 11.3 %reduce-scatter.31.cloned.1.call-done = bf16[128,512]{1,0:T(8,128)(2,1)} async-done(((bf16[512,512]{1,0:T(8,128)(2,1)}), bf16[128,512]{1,0:T(8,128)(2,1)}) %reduce-scatter.31.cloned.1.call-update) | async-done | bytes 131088
  283.8 15.8 %all-to-all-done.7 = bf16[64,10,256]{2,1,0:T(8,128)(2,1)S(1)} async-done(((bf16[64,10,256]{2,1,0:T(8,128)(2,1)}), bf16[64,10,256]{2,1,0:T(8,128)(2,1)S(1)}, u32[]{:S(2)}, u32[]{:S(2)}) %all-to-all-start.7) | async-done | bytes 327712 | tf_op jit(solution)/shard_map/all_to_all | solution.py:69
  306.2 12.6 %all_gather.34 = bf16[2,256,256]{2,1,0:T(8,128)(2,1)S(1)} all-gather(bf16[2,64,256]{2,1,0:T(8,128)(2,1)S(1)} %bitcast.265), channel_id=1, replica_groups=mesh['leaf'=64,'grid'=4] {'grid'}, dimensions={1}, use_global_device_ids=true | all-gather | bytes 327680 | tf_op jit(solution)/shard_map/all_gather | solution.py:11
  319.9 12.3 %all_gather.35 = bf16[2,256,256]{2,1,0:T(8,128)(2,1)S(1)} all-gather(bf16[2,64,256]{2,1,0:T(8,128)(2,1)S(1)} %fusion.4), channel_id=1, replica_groups=mesh['leaf'=64,'grid'=4] {'grid'}, dimensions={1}, use_global_device_ids=true | all-gather | bytes 327680 | tf_op jit(solution)/shard_map/all_gather | solution.py:11
  343.3 16.6 %all-to-all-done.8 = bf16[64,10,256]{2,1,0:T(8,128)(2,1)S(1)} async-done(((bf16[64,10,256]{2,1,0:T(8,128)(2,1)}), bf16[64,10,256]{2,1,0:T(8,128)(2,1)S(1)}, u32[]{:S(2)}, u32[]{:S(2)}) %all-to-all-start.8) | async-done | bytes 327712 | tf_op jit(solution)/shard_map/all_to_all | solution.py:26
  362.3 19.6 %reduce-scatter.17.cloned.1.call-done = bf16[64,2,256]{2,0,1:T(8,128)(2,1)} async-done(((bf16[256,2,256]{2,0,1:T(8,128)(2,1)}), bf16[64,2,256]{2,0,1:T(8,128)(2,1)}) %reduce-scatter.17.cloned.1.call-update) | async-done | bytes 65552 | tf_op jit(solution)/shard_map/reduce_scatter | solution.py:17
  382.7 12.3 %all_gather.36 = bf16[2,256,256]{2,1,0:T(8,128)(2,1)S(1)} all-gather(bf16[2,64,256]{2,1,0:T(8,128)(2,1)S(1)} %fusion.21), channel_id=1, replica_groups=mesh['leaf'=64,'grid'=4] {'grid'}, dimensions={1}, use_global_device_ids=true | all-gather | bytes 327680 | tf_op jit(solution)/shard_map/all_gather | solution.py:11
  409.5 16.6 %all-to-all-done.9 = bf16[64,10,256]{2,1,0:T(8,128)(2,1)S(1)} async-done(((bf16[64,10,256]{2,1,0:T(8,128)(2,1)}), bf16[64,10,256]{2,1,0:T(8,128)(2,1)S(1)}, u32[]{:S(2)}, u32[]{:S(2)}) %all-to-all-start.9) | async-done | bytes 327712 | tf_op jit(solution)/shard_map/all_to_all | solution.py:26
  428.5 19.6 %reduce-scatter.19.cloned.1.call-done = bf16[64,2,256]{2,0,1:T(8,128)(2,1)} async-done(((bf16[256,2,256]{2,0,1:T(8,128)(2,1)}), bf16[64,2,256]{2,0,1:T(8,128)(2,1)}) %reduce-scatter.19.cloned.1.call-update) | async-done | bytes 65552 | tf_op jit(solution)/shard_map/reduce_scatter | solution.py:17
  448.9 12.3 %all_gather.37 = bf16[2,256,256]{2,1,0:T(8,128)(2,1)S(1)} all-gather(bf16[2,64,256]{2,1,0:T(8,128)(2,1)S(1)} %fusion.19), channel_id=1, replica_groups=mesh['leaf'=64,'grid'=4] {'grid'}, dimensions={1}, use_global_device_ids=true | all-gather | bytes 327680 | tf_op jit(solution)/shard_map/all_gather | solution.py:11
  475.7 16.6 %all-to-all-done.10 = bf16[64,10,256]{2,1,0:T(8,128)(2,1)S(1)} async-done(((bf16[64,10,256]{2,1,0:T(8,128)(2,1)}), bf16[64,10,256]{2,1,0:T(8,128)(2,1)S(1)}, u32[]{:S(2)}, u32[]{:S(2)}) %all-to-all-start.10) | async-done | bytes 327712 | tf_op jit(solution)/shard_map/all_to_all | solution.py:26
  494.6 19.6 %reduce-scatter.21.cloned.1.call-done = bf16[64,2,256]{2,0,1:T(8,128)(2,1)} async-done(((bf16[256,2,256]{2,0,1:T(8,128)(2,1)}), bf16[64,2,256]{2,0,1:T(8,128)(2,1)}) %reduce-scatter.21.cloned.1.call-update) | async-done | bytes 65552 | tf_op jit(solution)/shard_map/reduce_scatter | solution.py:17
  515.1 12.3 %all_gather.38 = bf16[2,256,256]{2,1,0:T(8,128)(2,1)S(1)} all-gather(bf16[2,64,256]{2,1,0:T(8,128)(2,1)S(1)} %fusion.17), channel_id=1, replica_groups=mesh['leaf'=64,'grid'=4] {'grid'}, dimensions={1}, use_global_device_ids=true | all-gather | bytes 327680 | tf_op jit(solution)/shard_map/all_gather | solution.py:11
  541.8 16.6 %all-to-all-done.11 = bf16[64,10,256]{2,1,0:T(8,128)(2,1)S(1)} async-done(((bf16[64,10,256]{2,1,0:T(8,128)(2,1)}), bf16[64,10,256]{2,1,0:T(8,128)(2,1)S(1)}, u32[]{:S(2)}, u32[]{:S(2)}) %all-to-all-start.11) | async-done | bytes 327712 | tf_op jit(solution)/shard_map/all_to_all | solution.py:26
  560.8 19.6 %reduce-scatter.23.cloned.1.call-done = bf16[64,2,256]{2,0,1:T(8,128)(2,1)} async-done(((bf16[256,2,256]{2,0,1:T(8,128)(2,1)}), bf16[64,2,256]{2,0,1:T(8,128)(2,1)}) %reduce-scatter.23.cloned.1.call-update) | async-done | bytes 65552 | tf_op jit(solution)/shard_map/reduce_scatter | solution.py:17
  581.2 12.3 %all_gather.39 = bf16[2,256,256]{2,1,0:T(8,128)(2,1)S(1)} all-gather(bf16[2,64,256]{2,1,0:T(8,128)(2,1)S(1)} %fusion.15), channel_id=1, replica_groups=mesh['leaf'=64,'grid'=4] {'grid'}, dimensions={1}, use_global_device_ids=true | all-gather | bytes 327680 | tf_op jit(solution)/shard_map/all_gather | solution.py:11
  (210 shorter events, 232.9 us)
Async XLA Ops:
  6.5 14.4 %copy-start.1 = (bf16[4,2,64,512]{3,2,1,0:T(8,128)(2,1)S(1)}, bf16[4,2,64,512]{3,2,1,0:T(8,128)(2,1)}, u32[]{:S(2)}) copy-start(bf16[4,2,64,512]{3,2,1,0:T(8,128)(2,1)} %param.20) | copy-start | bytes 1572868
  6.5 42.5 %reduce-scatter.25.cloned.1.call-start = ((), (), s32[]{:S(2)}) async-start(), calls=%async_computation.24 | async-start | bytes 655360
  33.2 20.7 %all-to-all-start = ((s32[64,1,10]{2,1,0:T(1,128)}), s32[64,1,10]{2,1,0:T(1,128)S(1)}, u32[]{:S(2)}, u32[]{:S(2)}) async-start(s32[64,1,10]{2,1,0:T(1,128)} %bitcast.8), calls=%async_computation | async-start | bytes 65536 | tf_op jit(solution)/shard_map/all_to_all | solution.py:76
  52.9 10.8 %copy-start.3 = (bf16[5,2,64,256]{3,2,1,0:T(8,128)(2,1)S(1)}, bf16[5,2,64,256]{3,2,1,0:T(8,128)(2,1)}, u32[]{:S(2)}) copy-start(bf16[5,2,64,256]{3,2,1,0:T(8,128)(2,1)} %param.17) | copy-start | bytes 983044
  53.9 26.4 %all-to-all-start.1 = ((bf16[64,10,256]{2,1,0:T(8,128)(2,1)}), bf16[64,10,256]{2,1,0:T(8,128)(2,1)S(1)}, u32[]{:S(2)}, u32[]{:S(2)}) async-start(bf16[64,10,256]{2,1,0:T(8,128)(2,1)} %convert_element_type.212), calls=%async_computation.1 | async-start | bytes 1048576 | tf_op jit(solution)/shard_map/all_to_all | solution.py:69
  63.6 58.5 %reduce-scatter.27.cloned.1.call-start = ((), (), s32[]{:S(2)}) async-start(), calls=%async_computation.25 | async-start | bytes 655360
  103.9 22.2 %all-to-all-start.2 = ((s32[64,1,10]{2,1,0:T(1,128)}), s32[64,1,10]{2,1,0:T(1,128)S(1)}, u32[]{:S(2)}, u32[]{:S(2)}) async-start(s32[64,1,10]{2,1,0:T(1,128)} %bitcast.20), calls=%async_computation.2 | async-start | bytes 65536 | tf_op jit(solution)/shard_map/all_to_all | solution.py:76
  126.0 27.3 %all-to-all-start.3 = ((bf16[64,10,256]{2,1,0:T(8,128)(2,1)}), bf16[64,10,256]{2,1,0:T(8,128)(2,1)S(1)}, u32[]{:S(2)}, u32[]{:S(2)}) async-start(bf16[64,10,256]{2,1,0:T(8,128)(2,1)} %convert_element_type.221), calls=%async_computation.3 | async-start | bytes 1048576 | tf_op jit(solution)/shard_map/all_to_all | solution.py:69
  136.7 58.5 %reduce-scatter.29.cloned.1.call-start = ((), (), s32[]{:S(2)}) async-start(), calls=%async_computation.26 | async-start | bytes 655360
  176.9 22.2 %all-to-all-start.4 = ((s32[64,1,10]{2,1,0:T(1,128)}), s32[64,1,10]{2,1,0:T(1,128)S(1)}, u32[]{:S(2)}, u32[]{:S(2)}) async-start(s32[64,1,10]{2,1,0:T(1,128)} %bitcast.33), calls=%async_computation.4 | async-start | bytes 65536 | tf_op jit(solution)/shard_map/all_to_all | solution.py:76
  199.1 27.4 %all-to-all-start.5 = ((bf16[64,10,256]{2,1,0:T(8,128)(2,1)}), bf16[64,10,256]{2,1,0:T(8,128)(2,1)S(1)}, u32[]{:S(2)}, u32[]{:S(2)}) async-start(bf16[64,10,256]{2,1,0:T(8,128)(2,1)} %convert_element_type.230), calls=%async_computation.5 | async-start | bytes 1048576 | tf_op jit(solution)/shard_map/all_to_all | solution.py:69
  209.8 58.5 %reduce-scatter.31.cloned.1.call-start = ((), (), s32[]{:S(2)}) async-start(), calls=%async_computation.27 | async-start | bytes 655360
  250.1 22.2 %all-to-all-start.6 = ((s32[64,1,10]{2,1,0:T(1,128)}), s32[64,1,10]{2,1,0:T(1,128)S(1)}, u32[]{:S(2)}, u32[]{:S(2)}) async-start(s32[64,1,10]{2,1,0:T(1,128)} %bitcast.46), calls=%async_computation.6 | async-start | bytes 65536 | tf_op jit(solution)/shard_map/all_to_all | solution.py:76
  272.3 27.4 %all-to-all-start.7 = ((bf16[64,10,256]{2,1,0:T(8,128)(2,1)}), bf16[64,10,256]{2,1,0:T(8,128)(2,1)S(1)}, u32[]{:S(2)}, u32[]{:S(2)}) async-start(bf16[64,10,256]{2,1,0:T(8,128)(2,1)} %convert_element_type.239), calls=%async_computation.7 | async-start | bytes 1048576 | tf_op jit(solution)/shard_map/all_to_all | solution.py:69
  318.8 13.3 %copy-start.4 = (bf16[5,2,64,256]{3,2,1,0:T(8,128)(2,1)S(1)}, bf16[5,2,64,256]{3,2,1,0:T(8,128)(2,1)}, u32[]{:S(2)}) copy-start(bf16[5,2,64,256]{3,2,1,0:T(8,128)(2,1)} %param.19) | copy-start | bytes 983044
  336.0 23.8 %all-to-all-start.8 = ((bf16[64,10,256]{2,1,0:T(8,128)(2,1)}), bf16[64,10,256]{2,1,0:T(8,128)(2,1)S(1)}, u32[]{:S(2)}, u32[]{:S(2)}) async-start(bf16[64,10,256]{2,1,0:T(8,128)(2,1)} %reshape.581), calls=%async_computation.8 | async-start | bytes 1048576 | tf_op jit(solution)/shard_map/all_to_all | solution.py:26
  343.2 38.7 %reduce-scatter.17.cloned.1.call-start = ((), (), s32[]{:S(2)}) async-start(), calls=%async_computation.20 | async-start | bytes 327680 | tf_op jit(solution)/shard_map/reduce_scatter | solution.py:17
  360.0 1.2 copy-start.2
  398.9 27.2 %all-to-all-start.9 = ((bf16[64,10,256]{2,1,0:T(8,128)(2,1)}), bf16[64,10,256]{2,1,0:T(8,128)(2,1)S(1)}, u32[]{:S(2)}, u32[]{:S(2)}) async-start(bf16[64,10,256]{2,1,0:T(8,128)(2,1)} %reshape.585), calls=%async_computation.10 | async-start | bytes 1048576 | tf_op jit(solution)/shard_map/all_to_all | solution.py:26
  409.4 38.6 %reduce-scatter.19.cloned.1.call-start = ((), (), s32[]{:S(2)}) async-start(), calls=%async_computation.21 | async-start | bytes 327680 | tf_op jit(solution)/shard_map/reduce_scatter | solution.py:17
  465.0 27.2 %all-to-all-start.10 = ((bf16[64,10,256]{2,1,0:T(8,128)(2,1)}), bf16[64,10,256]{2,1,0:T(8,128)(2,1)S(1)}, u32[]{:S(2)}, u32[]{:S(2)}) async-start(bf16[64,10,256]{2,1,0:T(8,128)(2,1)} %reshape.589), calls=%async_computation.12 | async-start | bytes 1048576 | tf_op jit(solution)/shard_map/all_to_all | solution.py:26
  475.6 38.6 %reduce-scatter.21.cloned.1.call-start = ((), (), s32[]{:S(2)}) async-start(), calls=%async_computation.22 | async-start | bytes 327680 | tf_op jit(solution)/shard_map/reduce_scatter | solution.py:17
  531.2 27.2 %all-to-all-start.11 = ((bf16[64,10,256]{2,1,0:T(8,128)(2,1)}), bf16[64,10,256]{2,1,0:T(8,128)(2,1)S(1)}, u32[]{:S(2)}, u32[]{:S(2)}) async-start(bf16[64,10,256]{2,1,0:T(8,128)(2,1)} %reshape.593), calls=%async_computation.14 | async-start | bytes 1048576 | tf_op jit(solution)/shard_map/all_to_all | solution.py:26
  541.8 38.6 %reduce-scatter.23.cloned.1.call-start = ((), (), s32[]{:S(2)}) async-start(), calls=%async_computation.23 | async-start | bytes 327680 | tf_op jit(solution)/shard_map/reduce_scatter | solution.py:17
  (12 other events, 7.8 us)
Sparse Core Ops, SparseCore 0:
  22.5 26.4 reduce-scatter.24
  101.8 20.2 reduce-scatter.26
  174.9 20.2 reduce-scatter.28
  248.0 20.2 reduce-scatter.30
  362.4 19.4 reduce-scatter.16
  428.6 19.4 reduce-scatter.18
  494.7 19.4 reduce-scatter.20
  560.9 19.4 reduce-scatter.22
where the time goes:
time: 611 us; the launch traced here: 601 us
  waiting for transfers between devices  245 us (40%)
  blocking collectives  124 us (20%)
  starting transfers between devices  115 us (19%)
  local copies, waits for them, and re-layouts  56.7 us (9%)
  other arithmetic  35.3 us (6%)
  between operations  14.5 us (2%)
  matrix products  11.2 us (2%)
    all_gather x10, blocking collectives, apply_inverse(): lax.all_gather(block_bf, 'grid', axis=1, tiled=True)  124 us
    reduce_scatter x4, waiting for transfers between devices, grid_reduce(): lax.psum_scatter(term_fn(jnp.int32(0), kept_rows * lax.axis_size('grid'))...  78.4 us
    all_to_all x4, waiting for transfers between devices, send_back(): lax.all_to_all(solved_rows, 'leaf', split_axis=0, concat_axis=0, tiled=True)  66.4 us
    all_to_all x4, waiting for transfers between devices, local(): lax.all_to_all(outgoing.reshape(owners, capacity, columns).astype(jnp.bfl...  62 us
    all_to_all x4, starting transfers between devices, local(): lax.all_to_all(outgoing.reshape(owners, capacity, columns).astype(jnp.bfl...  41.7 us
    all_to_all x4, starting transfers between devices, send_back(): lax.all_to_all(solved_rows, 'leaf', split_axis=0, concat_axis=0, tiled=True)  38.8 us
    unnamed x12, waiting for transfers between devices  37.3 us
    all_to_all x4, starting transfers between devices, local(): lax.all_to_all(outgoing_index.reshape(owners, capacity), 'leaf', split_ax...  33.4 us
  transfers between devices with their start and end apart: 20, of which 17 were waited for; matrix products, arithmetic and copies ran while one was open for 5% of the time, Pallas kernels for 0%

commit v1 on v0

--- a/solution.py
+++ b/solution.py
@@ -8,7 +8,9 @@
     return jnp.einsum(
         "kiw,kwn->kin",
         inverse_rows,
-        lax.all_gather(block_bf, "grid", axis=1, tiled=True),
+        jnp.concatenate(
+            lax.all_to_all(jnp.stack([block_bf] * lax.axis_size("grid")), "grid", 0, 0), axis=1
+        ),
         preferred_element_type=jnp.float32,
     )
 

time: 611 us -> 586 us (0.959)
  blocking collectives: 124 us -> 49.8 us
  waiting for transfers between devices: 245 us -> 275 us
  starting transfers between devices: 115 us -> 130 us
    all_gather x10 -> x0, blocking collectives: 124 us -> none  [apply_inverse(): lax.all_gather(block_bf, 'grid', axis=1, tiled=True)]
    all_to_all x0 -> x5, blocking collectives: none -> 49.8 us  [apply_inverse(): lax.all_to_all(jnp.stack([block_bf] * lax.axis_size('grid')), 'grid', 0, 0)]
    all_to_all x0 -> x5, waiting for transfers between devices: none -> 30.9 us  [apply_inverse(): lax.all_to_all(jnp.stack([block_bf] * lax.axis_size('grid')), 'grid', 0, 0)]
    all_to_all x0 -> x5, starting transfers between devices: none -> 18.1 us  [apply_inverse(): lax.all_to_all(jnp.stack([block_bf] * lax.axis_size('grid')), 'grid', 0, 0)]
  transfers between devices with their start and end apart: 20 -> 25, of which waited for: 17 -> 21; matrix products, arithmetic and copies ran while one was open for 5% -> 5% of each run, Pallas kernels for 0% -> 0%
where the time goes in v1:
time: 586 us; the launch traced here: 576 us
  waiting for transfers between devices  275 us (47%)
  starting transfers between devices  130 us (22%)
  local copies, waits for them, and re-layouts  59.9 us (10%)
  blocking collectives  49.8 us (8%)
  other arithmetic  35.3 us (6%)
  between operations  14.7 us (3%)
  matrix products  11.2 us (2%)
    reduce_scatter x4, waiting for transfers between devices, grid_reduce(): lax.psum_scatter(term_fn(jnp.int32(0), kept_rows * lax.axis_size('grid'))...  77.3 us
    all_to_all x4, waiting for transfers between devices, send_back(): lax.all_to_all(solved_rows, 'leaf', split_axis=0, concat_axis=0, tiled=True)  66.4 us
    all_to_all x4, waiting for transfers between devices, local(): lax.all_to_all(outgoing.reshape(owners, capacity, columns).astype(jnp.bfl...  62 us
    all_to_all x5, blocking collectives, apply_inverse(): lax.all_to_all(jnp.stack([block_bf] * lax.axis_size('grid')), 'grid', 0, 0)  49.8 us
    all_to_all x4, starting transfers between devices, local(): lax.all_to_all(outgoing.reshape(owners, capacity, columns).astype(jnp.bfl...  42.7 us
    unnamed x12, waiting for transfers between devices  38.1 us
    all_to_all x4, starting transfers between devices, send_back(): lax.all_to_all(solved_rows, 'leaf', split_axis=0, concat_axis=0, tiled=True)  37.9 us
    all_to_all x5, waiting for transfers between devices, apply_inverse(): lax.all_to_all(jnp.stack([block_bf] * lax.axis_size('grid')), 'grid', 0, 0)  30.9 us
  transfers between devices with their start and end apart: 25, of which 21 were waited for; matrix products, arithmetic and copies ran while one was open for 5% of the time, Pallas kernels for 0%

profile of v1, /device:TPU:8, one launch (start us, length us, event | category | flops | bytes accessed | tf_op | source)
XLA Modules:
  0.0 575.7 jit_solution(9912033154459736082)
XLA Ops:
  29.6 12.1 %all-to-all-start = ((s32[64,1,10]{2,1,0:T(1,128)}), s32[64,1,10]{2,1,0:T(1,128)S(1)}, u32[]{:S(2)}, u32[]{:S(2)}) async-start(s32[64,1,10]{2,1,0:T(1,128)} %bitcast.8), calls=%async_computation | async-start | bytes 65536 | tf_op jit(solution)/shard_map/all_to_all | solution.py:78
  50.8 10.7 %all-to-all-start.2 = ((bf16[64,10,256]{2,1,0:T(8,128)(2,1)}), bf16[64,10,256]{2,1,0:T(8,128)(2,1)S(1)}, u32[]{:S(2)}, u32[]{:S(2)}) async-start(bf16[64,10,256]{2,1,0:T(8,128)(2,1)} %convert_element_type.217), calls=%async_computation.2 | async-start | bytes 1048576 | tf_op jit(solution)/shard_map/all_to_all | solution.py:71
  63.1 15.1 %all-to-all-done.2 = bf16[64,10,256]{2,1,0:T(8,128)(2,1)S(1)} async-done(((bf16[64,10,256]{2,1,0:T(8,128)(2,1)}), bf16[64,10,256]{2,1,0:T(8,128)(2,1)S(1)}, u32[]{:S(2)}, u32[]{:S(2)}) %all-to-all-start.2) | async-done | bytes 327712 | tf_op jit(solution)/shard_map/all_to_all | solution.py:71
  105.9 10.8 %reduce-scatter.27.cloned.1.call-done = bf16[128,512]{1,0:T(8,128)(2,1)} async-done(((bf16[512,512]{1,0:T(8,128)(2,1)}), bf16[128,512]{1,0:T(8,128)(2,1)}) %reduce-scatter.27.cloned.1.call-update) | async-done | bytes 131088
  120.5 10.7 %all-to-all-start.5 = ((bf16[64,10,256]{2,1,0:T(8,128)(2,1)}), bf16[64,10,256]{2,1,0:T(8,128)(2,1)S(1)}, u32[]{:S(2)}, u32[]{:S(2)}) async-start(bf16[64,10,256]{2,1,0:T(8,128)(2,1)} %convert_element_type.226), calls=%async_computation.5 | async-start | bytes 1048576 | tf_op jit(solution)/shard_map/all_to_all | solution.py:71
  132.1 15.7 %all-to-all-done.5 = bf16[64,10,256]{2,1,0:T(8,128)(2,1)S(1)} async-done(((bf16[64,10,256]{2,1,0:T(8,128)(2,1)}), bf16[64,10,256]{2,1,0:T(8,128)(2,1)S(1)}, u32[]{:S(2)}, u32[]{:S(2)}) %all-to-all-start.5) | async-done | bytes 327712 | tf_op jit(solution)/shard_map/all_to_all | solution.py:71
  175.3 11.0 %reduce-scatter.29.cloned.1.call-done = bf16[128,512]{1,0:T(8,128)(2,1)} async-done(((bf16[512,512]{1,0:T(8,128)(2,1)}), bf16[128,512]{1,0:T(8,128)(2,1)}) %reduce-scatter.29.cloned.1.call-update) | async-done | bytes 131088
  190.2 10.7 %all-to-all-start.8 = ((bf16[64,10,256]{2,1,0:T(8,128)(2,1)}), bf16[64,10,256]{2,1,0:T(8,128)(2,1)S(1)}, u32[]{:S(2)}, u32[]{:S(2)}) async-start(bf16[64,10,256]{2,1,0:T(8,128)(2,1)} %convert_element_type.235), calls=%async_computation.8 | async-start | bytes 1048576 | tf_op jit(solution)/shard_map/all_to_all | solution.py:71
  202.2 15.3 %all-to-all-done.8 = bf16[64,10,256]{2,1,0:T(8,128)(2,1)S(1)} async-done(((bf16[64,10,256]{2,1,0:T(8,128)(2,1)}), bf16[64,10,256]{2,1,0:T(8,128)(2,1)S(1)}, u32[]{:S(2)}, u32[]{:S(2)}) %all-to-all-start.8) | async-done | bytes 327712 | tf_op jit(solution)/shard_map/all_to_all | solution.py:71
  245.0 11.0 %reduce-scatter.31.cloned.1.call-done = bf16[128,512]{1,0:T(8,128)(2,1)} async-done(((bf16[512,512]{1,0:T(8,128)(2,1)}), bf16[128,512]{1,0:T(8,128)(2,1)}) %reduce-scatter.31.cloned.1.call-update) | async-done | bytes 131088
  259.8 10.6 %all-to-all-start.11 = ((bf16[64,10,256]{2,1,0:T(8,128)(2,1)}), bf16[64,10,256]{2,1,0:T(8,128)(2,1)S(1)}, u32[]{:S(2)}, u32[]{:S(2)}) async-start(bf16[64,10,256]{2,1,0:T(8,128)(2,1)} %convert_element_type.244), calls=%async_computation.11 | async-start | bytes 1048576 | tf_op jit(solution)/shard_map/all_to_all | solution.py:71
  271.4 15.8 %all-to-all-done.11 = bf16[64,10,256]{2,1,0:T(8,128)(2,1)S(1)} async-done(((bf16[64,10,256]{2,1,0:T(8,128)(2,1)}), bf16[64,10,256]{2,1,0:T(8,128)(2,1)S(1)}, u32[]{:S(2)}, u32[]{:S(2)}) %all-to-all-start.11) | async-done | bytes 327712 | tf_op jit(solution)/shard_map/all_to_all | solution.py:71
  293.8 10.3 %all_to_all.133 = bf16[4,2,64,256]{3,2,1,0:T(8,128)(2,1)S(1)} all-to-all(bf16[4,2,64,256]{3,2,1,0:T(8,128)(2,1)S(1)} %stack.27), channel_id=1, replica_groups=mesh['leaf'=64,'grid'=4] {'grid'}, dimensions={0} | all-to-all | bytes 524288 | tf_op jit(solution)/shard_map/all_to_all | solution.py:12
  326.0 16.6 %all-to-all-done.14 = bf16[64,10,256]{2,1,0:T(8,128)(2,1)S(1)} async-done(((bf16[64,10,256]{2,1,0:T(8,128)(2,1)}), bf16[64,10,256]{2,1,0:T(8,128)(2,1)S(1)}, u32[]{:S(2)}, u32[]{:S(2)}) %all-to-all-start.14) | async-done | bytes 327712 | tf_op jit(solution)/shard_map/all_to_all | solution.py:28
  345.0 19.3 %reduce-scatter.17.cloned.1.call-done = bf16[64,2,256]{2,0,1:T(8,128)(2,1)} async-done(((bf16[256,2,256]{2,0,1:T(8,128)(2,1)}), bf16[64,2,256]{2,0,1:T(8,128)(2,1)}) %reduce-scatter.17.cloned.1.call-update) | async-done | bytes 65552 | tf_op jit(solution)/shard_map/reduce_scatter | solution.py:19
  379.8 10.6 %all-to-all-start.16 = ((bf16[64,10,256]{2,1,0:T(8,128)(2,1)}), bf16[64,10,256]{2,1,0:T(8,128)(2,1)S(1)}, u32[]{:S(2)}, u32[]{:S(2)}) async-start(bf16[64,10,256]{2,1,0:T(8,128)(2,1)} %reshape.681), calls=%async_computation.17 | async-start | bytes 1048576 | tf_op jit(solution)/shard_map/all_to_all | solution.py:28
  390.5 16.6 %all-to-all-done.16 = bf16[64,10,256]{2,1,0:T(8,128)(2,1)S(1)} async-done(((bf16[64,10,256]{2,1,0:T(8,128)(2,1)}), bf16[64,10,256]{2,1,0:T(8,128)(2,1)S(1)}, u32[]{:S(2)}, u32[]{:S(2)}) %all-to-all-start.16) | async-done | bytes 327712 | tf_op jit(solution)/shard_map/all_to_all | solution.py:28
  409.4 19.3 %reduce-scatter.19.cloned.1.call-done = bf16[64,2,256]{2,0,1:T(8,128)(2,1)} async-done(((bf16[256,2,256]{2,0,1:T(8,128)(2,1)}), bf16[64,2,256]{2,0,1:T(8,128)(2,1)}) %reduce-scatter.19.cloned.1.call-update) | async-done | bytes 65552 | tf_op jit(solution)/shard_map/reduce_scatter | solution.py:19
  444.3 10.6 %all-to-all-start.18 = ((bf16[64,10,256]{2,1,0:T(8,128)(2,1)}), bf16[64,10,256]{2,1,0:T(8,128)(2,1)S(1)}, u32[]{:S(2)}, u32[]{:S(2)}) async-start(bf16[64,10,256]{2,1,0:T(8,128)(2,1)} %reshape.687), calls=%async_computation.20 | async-start | bytes 1048576 | tf_op jit(solution)/shard_map/all_to_all | solution.py:28
  454.9 16.6 %all-to-all-done.18 = bf16[64,10,256]{2,1,0:T(8,128)(2,1)S(1)} async-done(((bf16[64,10,256]{2,1,0:T(8,128)(2,1)}), bf16[64,10,256]{2,1,0:T(8,128)(2,1)S(1)}, u32[]{:S(2)}, u32[]{:S(2)}) %all-to-all-start.18) | async-done | bytes 327712 | tf_op jit(solution)/shard_map/all_to_all | solution.py:28
  473.9 19.3 %reduce-scatter.21.cloned.1.call-done = bf16[64,2,256]{2,0,1:T(8,128)(2,1)} async-done(((bf16[256,2,256]{2,0,1:T(8,128)(2,1)}), bf16[64,2,256]{2,0,1:T(8,128)(2,1)}) %reduce-scatter.21.cloned.1.call-update) | async-done | bytes 65552 | tf_op jit(solution)/shard_map/reduce_scatter | solution.py:19
  508.7 10.6 %all-to-all-start.20 = ((bf16[64,10,256]{2,1,0:T(8,128)(2,1)}), bf16[64,10,256]{2,1,0:T(8,128)(2,1)S(1)}, u32[]{:S(2)}, u32[]{:S(2)}) async-start(bf16[64,10,256]{2,1,0:T(8,128)(2,1)} %reshape.693), calls=%async_computation.23 | async-start | bytes 1048576 | tf_op jit(solution)/shard_map/all_to_all | solution.py:28
  519.3 16.6 %all-to-all-done.20 = bf16[64,10,256]{2,1,0:T(8,128)(2,1)S(1)} async-done(((bf16[64,10,256]{2,1,0:T(8,128)(2,1)}), bf16[64,10,256]{2,1,0:T(8,128)(2,1)S(1)}, u32[]{:S(2)}, u32[]{:S(2)}) %all-to-all-start.20) | async-done | bytes 327712 | tf_op jit(solution)/shard_map/all_to_all | solution.py:28
  538.3 19.3 %reduce-scatter.23.cloned.1.call-done = bf16[64,2,256]{2,0,1:T(8,128)(2,1)} async-done(((bf16[256,2,256]{2,0,1:T(8,128)(2,1)}), bf16[64,2,256]{2,0,1:T(8,128)(2,1)}) %reduce-scatter.23.cloned.1.call-update) | async-done | bytes 65552 | tf_op jit(solution)/shard_map/reduce_scatter | solution.py:19
  (234 shorter events, 225.8 us)
Async XLA Ops:
  8.1 11.1 %all-to-all-start.1 = ((bf16[4,2,64,256]{3,2,1,0:T(8,128)(2,1)}), bf16[4,2,64,256]{3,2,1,0:T(8,128)(2,1)S(1)}, u32[]{:S(2)}, u32[]{:S(2)}) async-start(bf16[4,2,64,256]{3,2,1,0:T(8,128)(2,1)} %stack.23), calls=%async_computation.1 | async-start | bytes 524288 | tf_op jit(solution)/shard_map/all_to_all | solution.py:12
  12.5 34.4 %reduce-scatter.25.cloned.1.call-start = ((), (), s32[]{:S(2)}) async-start(), calls=%async_computation.34 | async-start | bytes 655360
  29.6 21.3 %all-to-all-start = ((s32[64,1,10]{2,1,0:T(1,128)}), s32[64,1,10]{2,1,0:T(1,128)S(1)}, u32[]{:S(2)}, u32[]{:S(2)}) async-start(s32[64,1,10]{2,1,0:T(1,128)} %bitcast.8), calls=%async_computation | async-start | bytes 65536 | tf_op jit(solution)/shard_map/all_to_all | solution.py:78
  50.8 27.4 %all-to-all-start.2 = ((bf16[64,10,256]{2,1,0:T(8,128)(2,1)}), bf16[64,10,256]{2,1,0:T(8,128)(2,1)S(1)}, u32[]{:S(2)}, u32[]{:S(2)}) async-start(bf16[64,10,256]{2,1,0:T(8,128)(2,1)} %convert_element_type.217), calls=%async_computation.2 | async-start | bytes 1048576 | tf_op jit(solution)/shard_map/all_to_all | solution.py:71
  61.6 55.1 %reduce-scatter.27.cloned.1.call-start = ((), (), s32[]{:S(2)}) async-start(), calls=%async_computation.35 | async-start | bytes 655360
  99.5 21.0 %all-to-all-start.3 = ((s32[64,1,10]{2,1,0:T(1,128)}), s32[64,1,10]{2,1,0:T(1,128)S(1)}, u32[]{:S(2)}, u32[]{:S(2)}) async-start(s32[64,1,10]{2,1,0:T(1,128)} %bitcast.22), calls=%async_computation.3 | async-start | bytes 65536 | tf_op jit(solution)/shard_map/all_to_all | solution.py:78
  120.5 27.3 %all-to-all-start.5 = ((bf16[64,10,256]{2,1,0:T(8,128)(2,1)}), bf16[64,10,256]{2,1,0:T(8,128)(2,1)S(1)}, u32[]{:S(2)}, u32[]{:S(2)}) async-start(bf16[64,10,256]{2,1,0:T(8,128)(2,1)} %convert_element_type.226), calls=%async_computation.5 | async-start | bytes 1048576 | tf_op jit(solution)/shard_map/all_to_all | solution.py:71
  131.2 55.1 %reduce-scatter.29.cloned.1.call-start = ((), (), s32[]{:S(2)}) async-start(), calls=%async_computation.36 | async-start | bytes 655360
  169.2 21.0 %all-to-all-start.6 = ((s32[64,1,10]{2,1,0:T(1,128)}), s32[64,1,10]{2,1,0:T(1,128)S(1)}, u32[]{:S(2)}, u32[]{:S(2)}) async-start(s32[64,1,10]{2,1,0:T(1,128)} %bitcast.37), calls=%async_computation.6 | async-start | bytes 65536 | tf_op jit(solution)/shard_map/all_to_all | solution.py:78
  190.2 27.3 %all-to-all-start.8 = ((bf16[64,10,256]{2,1,0:T(8,128)(2,1)}), bf16[64,10,256]{2,1,0:T(8,128)(2,1)S(1)}, u32[]{:S(2)}, u32[]{:S(2)}) async-start(bf16[64,10,256]{2,1,0:T(8,128)(2,1)} %convert_element_type.235), calls=%async_computation.8 | async-start | bytes 1048576 | tf_op jit(solution)/shard_map/all_to_all | solution.py:71
  200.9 55.1 %reduce-scatter.31.cloned.1.call-start = ((), (), s32[]{:S(2)}) async-start(), calls=%async_computation.37 | async-start | bytes 655360
  238.8 21.0 %all-to-all-start.9 = ((s32[64,1,10]{2,1,0:T(1,128)}), s32[64,1,10]{2,1,0:T(1,128)S(1)}, u32[]{:S(2)}, u32[]{:S(2)}) async-start(s32[64,1,10]{2,1,0:T(1,128)} %bitcast.52), calls=%async_computation.9 | async-start | bytes 65536 | tf_op jit(solution)/shard_map/all_to_all | solution.py:78
  259.8 27.3 %all-to-all-start.11 = ((bf16[64,10,256]{2,1,0:T(8,128)(2,1)}), bf16[64,10,256]{2,1,0:T(8,128)(2,1)S(1)}, u32[]{:S(2)}, u32[]{:S(2)}) async-start(bf16[64,10,256]{2,1,0:T(8,128)(2,1)} %convert_element_type.244), calls=%async_computation.11 | async-start | bytes 1048576 | tf_op jit(solution)/shard_map/all_to_all | solution.py:71
  305.8 10.1 %all-to-all-start.13 = ((bf16[4,2,64,256]{3,2,1,0:T(8,128)(2,1)}), bf16[4,2,64,256]{3,2,1,0:T(8,128)(2,1)S(1)}, u32[]{:S(2)}, u32[]{:S(2)}) async-start(bf16[4,2,64,256]{3,2,1,0:T(8,128)(2,1)} %stack.28), calls=%async_computation.13 | async-start | bytes 524288 | tf_op jit(solution)/shard_map/all_to_all | solution.py:12
  319.8 22.8 %all-to-all-start.14 = ((bf16[64,10,256]{2,1,0:T(8,128)(2,1)}), bf16[64,10,256]{2,1,0:T(8,128)(2,1)S(1)}, u32[]{:S(2)}, u32[]{:S(2)}) async-start(bf16[64,10,256]{2,1,0:T(8,128)(2,1)} %reshape.675), calls=%async_computation.14 | async-start | bytes 1048576 | tf_op jit(solution)/shard_map/all_to_all | solution.py:28
  326.0 38.4 %reduce-scatter.17.cloned.1.call-start = ((), (), s32[]{:S(2)}) async-start(), calls=%async_computation.30 | async-start | bytes 327680 | tf_op jit(solution)/shard_map/reduce_scatter | solution.py:19
  379.8 27.3 %all-to-all-start.16 = ((bf16[64,10,256]{2,1,0:T(8,128)(2,1)}), bf16[64,10,256]{2,1,0:T(8,128)(2,1)S(1)}, u32[]{:S(2)}, u32[]{:S(2)}) async-start(bf16[64,10,256]{2,1,0:T(8,128)(2,1)} %reshape.681), calls=%async_computation.17 | async-start | bytes 1048576 | tf_op jit(solution)/shard_map/all_to_all | solution.py:28
  390.4 38.3 %reduce-scatter.19.cloned.1.call-start = ((), (), s32[]{:S(2)}) async-start(), calls=%async_computation.31 | async-start | bytes 327680 | tf_op jit(solution)/shard_map/reduce_scatter | solution.py:19
  430.3 10.1 %all-to-all-start.17 = ((bf16[4,2,64,256]{3,2,1,0:T(8,128)(2,1)}), bf16[4,2,64,256]{3,2,1,0:T(8,128)(2,1)S(1)}, u32[]{:S(2)}, u32[]{:S(2)}) async-start(bf16[4,2,64,256]{3,2,1,0:T(8,128)(2,1)} %stack.30), calls=%async_computation.19 | async-start | bytes 524288 | tf_op jit(solution)/shard_map/all_to_all | solution.py:12
  444.3 27.2 %all-to-all-start.18 = ((bf16[64,10,256]{2,1,0:T(8,128)(2,1)}), bf16[64,10,256]{2,1,0:T(8,128)(2,1)S(1)}, u32[]{:S(2)}, u32[]{:S(2)}) async-start(bf16[64,10,256]{2,1,0:T(8,128)(2,1)} %reshape.687), calls=%async_computation.20 | async-start | bytes 1048576 | tf_op jit(solution)/shard_map/all_to_all | solution.py:28
  454.9 38.3 %reduce-scatter.21.cloned.1.call-start = ((), (), s32[]{:S(2)}) async-start(), calls=%async_computation.32 | async-start | bytes 327680 | tf_op jit(solution)/shard_map/reduce_scatter | solution.py:19
  494.8 10.1 %all-to-all-start.19 = ((bf16[4,2,64,256]{3,2,1,0:T(8,128)(2,1)}), bf16[4,2,64,256]{3,2,1,0:T(8,128)(2,1)S(1)}, u32[]{:S(2)}, u32[]{:S(2)}) async-start(bf16[4,2,64,256]{3,2,1,0:T(8,128)(2,1)} %stack.31), calls=%async_computation.22 | async-start | bytes 524288 | tf_op jit(solution)/shard_map/all_to_all | solution.py:12
  508.7 27.2 %all-to-all-start.20 = ((bf16[64,10,256]{2,1,0:T(8,128)(2,1)}), bf16[64,10,256]{2,1,0:T(8,128)(2,1)S(1)}, u32[]{:S(2)}, u32[]{:S(2)}) async-start(bf16[64,10,256]{2,1,0:T(8,128)(2,1)} %reshape.693), calls=%async_computation.23 | async-start | bytes 1048576 | tf_op jit(solution)/shard_map/all_to_all | solution.py:28
  519.3 38.3 %reduce-scatter.23.cloned.1.call-start = ((), (), s32[]{:S(2)}) async-start(), calls=%async_computation.33 | async-start | bytes 327680 | tf_op jit(solution)/shard_map/reduce_scatter | solution.py:19
  (16 other events, 44.9 us)
Sparse Core Ops, SparseCore 0:
  21.7 25.1 reduce-scatter.24
  97.5 19.0 reduce-scatter.26
  167.1 19.1 reduce-scatter.28
  236.8 19.1 reduce-scatter.30
  345.1 19.1 reduce-scatter.16
  409.6 19.1 reduce-scatter.18
  474.0 19.1 reduce-scatter.20
  538.4 19.1 reduce-scatter.22
